TPU v7x, 32 devices: a whole 2x2x4 slice. The times are simulated.
32 devices in a mesh: dir: 8 (over y, x, core), freq: 4 (over z).
Axes of the slice: x: 2, y: 2, z: 4, core: 2. Of those that a mesh axis runs over, the one named last changes fastest.
Arguments:
- observed: float32 [512, 8, 2, 2, 512], P('dir', 'freq'), as said below
- flags: int32 [512, 2, 512], P('dir'), may hold values from 0 to 1, as said below
- screen: float32 [16, 512], P('dir'), may hold values from -6 to 6
- screen_kernel: float32 [512, 512], replicated
- station_uv: float32 [2, 2, 512], replicated, may hold values from -360 to 360
- source_lm: float32 [2, 3072], P(None, 'dir'), may hold values from -0.05 to 0.05
- source_flux: float32 [3072], P('dir')
- station_gain: bfloat16 [8, 2, 2, 512, 3072], P('freq', None, None, None, 'dir'), may hold values from -4.1875 to 4.1875
- source_direction: int32 [3072], P('dir'), may hold values from 0 to 1
- freq_ratio: float32 [8], P('freq')
Outputs:
- residual: float32 [512, 8, 2, 2, 512], P('dir', 'freq')
- updated_screen: float32 [16, 512], P('dir')
Inputs may be any that keep to these rules, and one draw needn't show every extreme that they name: observed is Hermitian in its stations: observed[p, f, t, 0, q] equals observed[q, f, t, 0, p] and observed[p, f, t, 1, q] equals minus observed[q, f, t, 1, p]. flags[p, t, q] equals flags[q, t, p].
All inputs are finite; a program needn't handle non-finite values.
Results may differ from a plain program's by a relative error of at most 0.0037.
Values may be sent and summed in bfloat16 or wider, within the bound.
A program may use at most 128 MiB of HBM per device.

v0:
```python
import math
import jax
import jax.numpy as jnp
from jax import lax
from jax.sharding import PartitionSpec as P

step_size = 0.3
epsilon = 1e-06
highest = lax.Precision.HIGHEST


def body(
    observed,
    flags,
    screen,
    screen_kernel,
    station_uv,
    source_lm,
    source_flux,
    station_gain,
    source_direction,
    freq_ratio,
):
    dir_count = lax.axis_size("dir")
    stations = screen.shape[1]
    local_dirs = screen.shape[0]
    local_sources = source_flux.shape[0]
    local_rows = observed.shape[0]
    channels = freq_ratio.shape[0]
    times_count = station_uv.shape[0]
    matrices = channels * times_count
    scaling = 1.0 / math.sqrt(local_sources * dir_count)
    onehot_dirs = (
        source_direction[:, None] == jnp.arange(local_dirs, dtype=jnp.int32)[None, :]
    ).astype(jnp.float32)
    screen_src = jnp.einsum("dp,kd->pk", screen, onehot_dirs, precision=highest)
    freq_each = jnp.repeat(freq_ratio, times_count)
    uv_each = jnp.tile(station_uv, (channels, 1, 1))
    geometry = jnp.einsum("mcp,ck->pmk", uv_each, source_lm, precision=highest)
    phase_angle = (
        screen_src[:, None, :] / freq_each[None, :, None]
        + (2.0 * math.pi * freq_each)[None, :, None] * geometry
    )
    gain_all = station_gain.reshape(matrices, 2, stations, local_sources).astype(jnp.float32)
    gain_re = jnp.transpose(gain_all[:, 0], (1, 0, 2))
    gain_im = jnp.transpose(gain_all[:, 1], (1, 0, 2))
    cosine = jnp.cos(phase_angle)
    sine = jnp.sin(phase_angle)
    amplitude = jnp.sqrt(source_flux)[None, None, :]
    phasor_re = (amplitude * (gain_re * cosine - gain_im * sine)).astype(jnp.bfloat16)
    phasor_im = (amplitude * (gain_re * sine + gain_im * cosine)).astype(jnp.bfloat16)
    left_mat = jnp.concatenate([phasor_re, phasor_im], axis=2)
    skew_mat = jnp.concatenate([phasor_im, -phasor_re], axis=2)
    real_part = jnp.einsum("pmk,qmk->pmq", left_mat, left_mat, preferred_element_type=jnp.float32)
    imag_part = jnp.einsum("pmk,qmk->pmq", skew_mat, left_mat, preferred_element_type=jnp.float32)
    packed_rows = lax.psum_scatter(
        (real_part + imag_part) * scaling, "dir", scatter_dimension=0, tiled=True
    )
    mirrored = lax.all_to_all(packed_rows, "dir", split_axis=2, concat_axis=0, tiled=True)
    mirrored = jnp.transpose(mirrored, (2, 1, 0))
    model_rows = jnp.stack([(packed_rows + mirrored) * 0.5, (packed_rows - mirrored) * 0.5], axis=2)
    row_ids = lax.axis_index("dir") * local_rows + jnp.arange(local_rows, dtype=jnp.int32)
    cross_baseline = (row_ids[:, None] != jnp.arange(stations, dtype=jnp.int32)[None, :]).astype(
        jnp.float32
    )
    baseline_keep = (
        jnp.tile(flags, (1, channels, 1)).astype(jnp.float32) * cross_baseline[:, None, :]
    )
    obs_rows = observed.reshape(local_rows, matrices, 2, stations)
    residual = baseline_keep[:, :, None, :] * (obs_rows - model_rows)
    resid_half = residual.astype(jnp.bfloat16)
    forward_mat = jnp.stack([left_mat, -skew_mat], axis=2)
    conj_mat = jnp.concatenate([phasor_re, -phasor_im], axis=2)
    dual_mat = jnp.concatenate([phasor_im, phasor_re], axis=2)
    adjoint_mat = jnp.stack([conj_mat, dual_mat], axis=2)
    rows_piece = lax.all_gather(resid_half, "dir", axis=0, tiled=True)
    row_part = jnp.einsum(
        "rmwq,qmwk->rmk", rows_piece, forward_mat, preferred_element_type=jnp.float32
    )
    col_total = jnp.einsum(
        "rmwp,rmwk->pmk", rows_piece, adjoint_mat, preferred_element_type=jnp.float32
    )
    weight_re = row_part[..., :local_sources] + col_total[..., :local_sources]
    weight_im = row_part[..., local_sources:] - col_total[..., local_sources:]
    source_grad = (
        phasor_im.astype(jnp.float32) * weight_re - phasor_re.astype(jnp.float32) * weight_im
    )
    source_grad = source_grad * (scaling / freq_each)[None, :, None]
    local_grad = jnp.einsum("pmk,kd->dp", source_grad, onehot_dirs, precision=highest)
    entry_count = local_dirs * dir_count * stations
    total_grad = lax.psum(local_grad, "freq")
    smooth = jnp.dot(total_grad, screen_kernel, precision=highest)
    total_sq = lax.psum(jnp.sum(smooth * smooth), "dir")
    updated = screen - step_size * smooth * lax.rsqrt(total_sq / entry_count + epsilon)
    return (residual.reshape(observed.shape), updated)


def solution(mesh):
    placed = (
        P("dir", "freq", None, None, None),
        P("dir", None, None),
        P("dir", None),
        P(),
        P(),
        P(None, "dir"),
        P("dir"),
        P("freq", None, None, None, "dir"),
        P("dir"),
        P("freq"),
    )
    return jax.shard_map(
        body,
        mesh=mesh,
        in_specs=placed,
        out_specs=(P("dir", "freq", None, None, None), P("dir", None)),
        check_vma=False,
    )
```

profile of v0, /device:TPU:0, one launch (start us, length us, event | category | flops | bytes accessed | tf_op | source)
XLA Modules:
  0.0 248.1 jit_solution(14236749292300200952)
XLA Ops:
  8.8 5.5 %copy.27 = f32[2,2,2,512,384]{3,4,1,0,2:T(8,128)} copy(bf16[2,2,2,512,384]{4,3,2,1,0:T(8,128)(2,1)} %param.17) | data formatting | bytes 9437184 | tf_op jit(solution)/shard_map/convert_element_type | solution.py:44
  14.9 14.2 %fusion.46 = (f32[512,4,384]{0,2,1:T(8,128)S(1)}, f32[512,4,384]{0,2,1:T(8,128)S(1)}) fusion(f32[4,2,512]{2,1,0:T(2,128)S(1)} %bitcast.86, f32[2,384]{1,0:T(2,128)S(1)} %copy-done.12, f32[4]{0:T(128)S(1)} %get-tuple-element.16, f32[4]{0:T(128)S(1)} %div.26, f32[512,384]{0,1:T(8,128)S(1)} %convolution_bitcast_fusion), kind=kOutput, calls=%fused_computation.68 | convolution fusion | flops 21233664 | bytes 7097376 | tf_op jit(solution)/shard_map/mcp,ck->pmk/dot_general | solution.py:39
  29.1 3.2 %fusion.45 = (bf16[512,4,384]{0,2,1:T(8,128)(2,1)}, bf16[512,4,384]{0,2,1:T(8,128)(2,1)S(1)}, bf16[512,4,1,384]{0,3,1,2:T(8,128)(2,1)}, bf16[512,4,384]{0,2,1:T(8,128)(2,1)S(1)}) fusion(f32[512,4,384]{0,2,1:T(8,128)S(1)} %get-tuple-element.10, f32[4,2,512,384]{2,3,0,1:T(8,128)S(1)} %bitcast.78, f32[512,4,384]{0,2,1:T(8,128)S(1)} %get-tuple-element.11, ...), kind=kLoop, calls=%fused_computation.67 | loop fusion | flops 9437184 | bytes 18875904 | tf_op jit(solution)/shard_map/neg | solution.py:73
  32.6 2.1 fusion.30
  34.7 3.5 %multiply_bitcast_fusion = f32[512,4,512]{0,2,1:T(8,128)} fusion(f32[4,512,512]{2,1,0:T(8,128)S(1)} %fusion.30, bf16[512,4,384]{0,2,1:T(8,128)(2,1)S(1)} %get-tuple-element.5, bf16[512,4,384]{0,2,1:T(8,128)(2,1)S(1)} %neg.16, bf16[512,4,384]{0,2,1:T(8,128)(2,1)S(1)} %get-tuple-element.7), kind=kOutput, calls=%fused_computation.8 | convolution fusion | flops 1625292800 | bytes 13107200 | tf_op jit(solution)/shard_map/pmk,qmk->pmq/dot_general | solution.py:55
  38.1 5.5 %copy.32 = f32[512,4,512]{2,1,0:T(4,128)} copy(f32[512,4,512]{0,2,1:T(8,128)} %multiply_bitcast_fusion) | data formatting | bytes 8388608 | tf_op jit(solution)/shard_map/mul | solution.py:57
  47.3 80.0 %all-reduce.3.cloned.1.call-done = f32[512,4,512]{2,1,0:T(4,128)} async-done(((f32[512,4,512]{2,1,0:T(4,128)}), f32[512,4,512]{2,1,0:T(4,128)}) %all-reduce.3.cloned.1.call-update) | async-done | bytes 4194320
  129.7 3.0 %reshape.106 = f32[8,1,16384]{2,1,0:T(1,128)} reshape(f32[512,4,64]{2,1,0:T(4,128)} %bitcast.83) | data formatting | bytes 1048576
  132.7 3.5 %all-to-all-start = ((f32[8,1,16384]{2,1,0:T(1,128)}), f32[8,1,16384]{2,1,0:T(1,128)S(1)}, u32[]{:S(2)}, u32[]{:S(2)}) async-start(f32[8,1,16384]{2,1,0:T(1,128)} %reshape.106), calls=%async_computation | async-start | bytes 1048576 | tf_op jit(solution)/shard_map/all_to_all | solution.py:59
  136.5 2.0 broadcast_multiply_fusion
  138.5 7.4 %all-to-all-done = f32[8,1,16384]{2,1,0:T(1,128)S(1)} async-done(((f32[8,1,16384]{2,1,0:T(1,128)}), f32[8,1,16384]{2,1,0:T(1,128)S(1)}, u32[]{:S(2)}, u32[]{:S(2)}) %all-to-all-start) | async-done | bytes 524320 | tf_op jit(solution)/shard_map/all_to_all | solution.py:59
  147.2 2.9 %reduce = f32[8,16384]{1,0:T(8,128)S(1)} reduce(f32[8,1,16384]{2,1,0:T(1,128)} %copy-done.7, f32[]{:T(128)} %broadcast.60), dimensions={1}, to_apply=%all_to_all.13.reduce_sub_computation | reduce | bytes 1048580 | tf_op jit(solution)/shard_map/all_to_all | solution.py:59
  151.8 2.8 %copy.64 = f32[64,4,8,64]{0,2,1,3:T(8,128)} copy(f32[64,4,8,64]{0,1,3,2:T(4,128)} %bitcast.84) | data formatting | bytes 1048576 | tf_op jit(solution)/shard_map/all_to_all | solution.py:59
  154.6 2.4 all_to_all.16
  162.0 4.4 %maximum_negate_fusion = bf16[512,4,1,768]{0,3,1,2:T(8,128)(2,1)} fusion(bf16[512,4,1,384]{0,3,1,2:T(8,128)(2,1)} %get-tuple-element.6, bf16[512,4,1,384]{0,3,1,2:T(8,128)(2,1)} %bitcast.79), kind=kLoop, calls=%fused_computation.29 | loop fusion | flops 7864320 | bytes 6291456 | tf_op jit(solution)/shard_map/neg | solution.py:72
  167.3 3.8 %fusion.29 = (bf16[512,4,1,768]{0,3,1,2:T(8,128)(2,1)}, bf16[512,4,1,768]{0,3,1,2:T(8,128)(2,1)}, bf16[512,4,1,768]{0,3,1,2:T(8,128)(2,1)}) fusion(bf16[512,4,384]{0,2,1:T(8,128)(2,1)S(1)} %copy-done.2, bf16[512,4,384]{0,2,1:T(8,128)(2,1)S(1)} %get-tuple-element.7, bf16[512,4,384]{0,2,1:T(8,128)(2,1)S(1)} %copy-done.4), kind=kLoop, calls=%fused_computation.34 | loop fusion | flops 17301504 | bytes 14155776 | tf_op jit(solution)/shard_map/stack | solution.py:72
  171.1 2.6 %stack.42 = f32[64,2,2,1,512]{4,3,2,1,0:T(1,128)} reshape(f32[64,4,512]{2,1,0:T(4,128)} %copy-done.5) | data formatting | bytes 1048576 | tf_op jit(solution)/shard_map/stack | solution.py:61
  175.2 3.9 %fusion.31 = f32[64,2,2,2,512]{4,3,2,1,0:T(2,128)} fusion(f32[64,2,2,2,512]{4,3,2,1,0:T(2,128)} %param.10, f32[64,2,2,1,512]{4,3,2,1,0:T(1,128)} %stack.43, f32[64,2,2,1,512]{4,3,2,1,0:T(1,128)} %stack.42, f32[64,2,2,512]{3,2,1,0:T(2,128)} %broadcast_multiply_fusion.1), kind=kLoop, calls=%fused_computation.38 | loop fusion | flops 786432 | bytes 3670016 | tf_op jit(solution)/shard_map/mul | solution.py:70
  179.1 18.7 %all-gather.2.cloned.1.call-done = bf16[512,4,2,512]{3,1,2,0:T(4,128)(2,1)} async-done(((bf16[64,4,2,512]{3,1,2,0:T(4,128)(2,1)}), bf16[512,4,2,512]{3,1,2,0:T(4,128)(2,1)}) %all-gather.2.cloned.1.call-update) | async-done | bytes 4194320 | tf_op jit(solution)/shard_map/all_gather | solution.py:76
  197.8 7.7 %fusion.24 = f32[512,4,768]{0,2,1:T(8,128)S(1)} fusion(bf16[512,4,2,512]{3,1,2,0:T(4,128)(2,1)} %all-gather.2.cloned.1.call-done, bf16[512,4,1,768]{0,3,1,2:T(8,128)(2,1)} %maximum_negate_fusion, bf16[512,4,1,768]{0,3,1,2:T(8,128)(2,1)} %get-tuple-element.8), kind=kOutput, calls=%fused_computation.33 | convolution fusion | flops 3224371200 | bytes 16777216 | tf_op jit(solution)/shard_map/rmwq,qmwk->rmk/dot_general | solution.py:77
  205.5 6.8 %fusion.19 = f32[512,4,768]{0,2,1:T(8,128)S(1)} fusion(bf16[512,4,2,512]{3,1,2,0:T(4,128)(2,1)} %all-gather.2.cloned.1.call-done, bf16[512,4,1,768]{0,3,1,2:T(8,128)(2,1)S(1)} %copy-done.6, bf16[512,4,1,768]{0,3,1,2:T(8,128)(2,1)} %get-tuple-element.12), kind=kOutput, calls=%fused_computation.32 | convolution fusion | flops 3224371200 | bytes 16777216 | tf_op jit(solution)/shard_map/rmwp,rmwk->pmk/dot_general | solution.py:80
  212.3 1.9 fusion.16
  214.7 11.7 %psum.14 = f32[2,512]{1,0:T(2,128)S(1)} all-reduce(f32[2,512]{1,0:T(2,128)S(1)} %fusion.36), channel_id=1, replica_groups=mesh['dir'=8,'freq'=4] {'freq'}, use_global_device_ids=true, to_apply=%region_2.0 | all-reduce | flops 1024 | bytes 8192 | tf_op jit(solution)/shard_map/psum | solution.py:91
  227.5 12.5 %psum.15 = f32[]{:T(128)} all-reduce(f32[]{:T(128)} %get-tuple-element.18), channel_id=1, replica_groups=mesh['dir'=8,'freq'=4] {'dir'}, use_global_device_ids=true, to_apply=%region_4.0 | all-reduce | flops 1 | bytes 8 | tf_op jit(solution)/shard_map/psum | solution.py:93
  (62 shorter events, 20.9 us)
Async XLA Ops:
  7.2 219.2 %copy-start = (f32[512,512]{1,0:T(8,128)S(1)}, f32[512,512]{1,0:T(8,128)}, u32[]{:S(2)}) copy-start(f32[512,512]{1,0:T(8,128)} %param.13) | copy-start | bytes 3145732
  7.2 120.1 %all-reduce.3.cloned.1.call-start = ((), (), s32[]{:S(2)}) async-start(), calls=%async_computation.2 | async-start | bytes 8388608
  8.8 5.5 %copy-start.9 = (f32[2,512]{1,0:T(2,128)S(1)}, f32[2,512]{1,0:T(2,128)}, u32[]{:S(2)}) copy-start(f32[2,512]{1,0:T(2,128)} %param.12) | copy-start | bytes 12292
  8.8 5.5 %copy-start.10 = (s32[384]{0:T(512)S(1)}, s32[384]{0:T(512)}, u32[]{:S(2)}) copy-start(s32[384]{0:T(512)} %param.18) | copy-start | bytes 4612
  8.8 6.0 %copy-start.11 = (f32[2,2,512]{2,1,0:T(2,128)S(1)}, f32[2,2,512]{2,1,0:T(2,128)}, u32[]{:S(2)}) copy-start(f32[2,2,512]{2,1,0:T(2,128)} %param.14) | copy-start | bytes 24580
  8.8 6.0 %copy-start.12 = (f32[2,384]{1,0:T(2,128)S(1)}, f32[2,384]{1,0:T(2,128)}, u32[]{:S(2)}) copy-start(f32[2,384]{1,0:T(2,128)} %param.15) | copy-start | bytes 9220
  14.8 14.2 %slice-start = ((s8[6291456]{0:T(1024)(128)(4,1)}), s8[4194304]{0:T(1024)(128)(4,1)S(1)}, s32[]{:S(2)}) async-start(s8[6291456]{0:T(1024)(128)(4,1)} %bitcast.76), calls=%async_computation.3 | async-start | bytes 8388608
  14.9 14.2 %slice-start.1 = ((s8[6291456]{0:T(1024)(128)(4,1)}), s8[2097152]{0:T(1024)(128)(4,1)S(1)}, s32[]{:S(2)}) async-start(s8[6291456]{0:T(1024)(128)(4,1)} %bitcast.76), calls=%async_computation.4 | async-start | bytes 4194304
  32.3 2.4 copy-start.1
  43.6 0.9 copy-start.8
  43.6 2.4 copy-start.13
  132.7 13.1 %all-to-all-start = ((f32[8,1,16384]{2,1,0:T(1,128)}), f32[8,1,16384]{2,1,0:T(1,128)S(1)}, u32[]{:S(2)}, u32[]{:S(2)}) async-start(f32[8,1,16384]{2,1,0:T(1,128)} %reshape.106), calls=%async_computation | async-start | bytes 1048576 | tf_op jit(solution)/shard_map/all_to_all | solution.py:59
  136.2 61.6 %all-gather.2.cloned.1.call-start = ((), (), s32[]{:S(2)}) async-start(), calls=%async_computation.1 | async-start | bytes 4718592 | tf_op jit(solution)/shard_map/all_gather | solution.py:76
  145.9 0.8 copy-start.7
  158.4 0.8 copy-start.5
  161.9 5.4 %copy-start.2 = (bf16[512,4,384]{0,2,1:T(8,128)(2,1)S(1)}, bf16[512,4,384]{0,2,1:T(8,128)(2,1)}, u32[]{:S(2)}) copy-start(bf16[512,4,384]{0,2,1:T(8,128)(2,1)} %copy-done.1) | copy-start | bytes 4718596
  162.0 5.4 %copy-start.4 = (bf16[512,4,384]{0,2,1:T(8,128)(2,1)S(1)}, bf16[512,4,384]{0,2,1:T(8,128)(2,1)}, u32[]{:S(2)}) copy-start(bf16[512,4,384]{0,2,1:T(8,128)(2,1)} %get-tuple-element.4) | copy-start | bytes 4718596
  197.8 7.8 %copy-start.6 = (bf16[512,4,1,768]{0,3,1,2:T(8,128)(2,1)S(1)}, bf16[512,4,1,768]{0,3,1,2:T(8,128)(2,1)}, u32[]{:S(2)}) copy-start(bf16[512,4,1,768]{0,3,1,2:T(8,128)(2,1)} %get-tuple-element.9) | copy-start | bytes 9437188
  205.5 6.8 %copy-start.3 = (bf16[512,4,384]{0,2,1:T(8,128)(2,1)S(1)}, bf16[512,4,384]{0,2,1:T(8,128)(2,1)}, u32[]{:S(2)}) copy-start(bf16[512,4,384]{0,2,1:T(8,128)(2,1)} %copy-done.1) | copy-start | bytes 4718596
Sparse Core Ops, SparseCore 0:
  43.8 83.5 all-reduce.2
  162.1 35.6 all-gather.1
where the time goes:
time: 249 us; the launch traced here: 248 us
  waiting for transfers between devices  106 us (43%)
  matrix products  36.4 us (15%)
  local copies, waits for them, and re-layouts  34.8 us (14%)
  other arithmetic  27.3 us (11%)
  blocking collectives  24.1 us (10%)
  between operations  15.6 us (6%)
  starting transfers between devices  3.75 us (2%)
    unnamed x3, waiting for transfers between devices  80.1 us
    all_gather x1, waiting for transfers between devices, body(): rows_piece = lax.all_gather(resid_half, 'dir', axis=0, tiled=True)  18.7 us
    dot_general x1, matrix products, body(): geometry = jnp.einsum('mcp,ck->pmk', uv_each, source_lm, precision=highest)  14.2 us
    psum x1, blocking collectives, body(): total_sq = lax.psum(jnp.sum(smooth * smooth), 'dir')  12.5 us
    psum x1, blocking collectives, body(): total_grad = lax.psum(local_grad, 'freq')  11.7 us
    unnamed x36, local copies, waits for them, and re-layouts  8.85 us
    dot_general x1, matrix products, body(): jnp.einsum('rmwq,qmwk->rmk', rows_piece, forward_mat, preferred_element_t...  7.74 us
    all_to_all x1, waiting for transfers between devices, body(): lax.all_to_all(packed_rows, 'dir', split_axis=2, concat_axis=0, tiled=True)  7.36 us
  transfers between devices with their start and end apart: 3, of which 3 were waited for; matrix products, arithmetic and copies ran while one was open for 9% of the time, Pallas kernels for 0%

commit v1 on v0

--- a/solution.py
+++ b/solution.py
@@ -56,7 +56,12 @@
     packed_rows = lax.psum_scatter(
         (real_part + imag_part) * scaling, "dir", scatter_dimension=0, tiled=True
     )
-    mirrored = lax.all_to_all(packed_rows, "dir", split_axis=2, concat_axis=0, tiled=True)
+    mirrored = jnp.concatenate(
+        lax.all_to_all(
+            jnp.stack(jnp.split(packed_rows, lax.axis_size("dir"), axis=2)), "dir", 0, 0
+        ),
+        axis=0,
+    )
     mirrored = jnp.transpose(mirrored, (2, 1, 0))
     model_rows = jnp.stack([(packed_rows + mirrored) * 0.5, (packed_rows - mirrored) * 0.5], axis=2)
     row_ids = lax.axis_index("dir") * local_rows + jnp.arange(local_rows, dtype=jnp.int32)

time: 249 us -> 258 us (1.036)
  local copies, waits for them, and re-layouts: 34.8 us -> 43.5 us
    unnamed x36 -> x40, local copies, waits for them, and re-layouts: 8.85 us -> 19 us
    all_to_all x3 -> x1, local copies, waits for them, and re-layouts: 5.69 us -> 0.51 us  [body(): lax.all_to_all(jnp.stack(jnp.split(packed_rows, lax.axis_size('dir'), axi...]
  transfers between devices with their start and end apart: 3 -> 3, of which waited for: 3 -> 3; matrix products, arithmetic and copies ran while one was open for 9% -> 8% of each run, Pallas kernels for 0% -> 0%
where the time goes in v1:
time: 258 us; the launch traced here: 257 us
  waiting for transfers between devices  106 us (41%)
  local copies, waits for them, and re-layouts  43.5 us (17%)
  matrix products  36.4 us (14%)
  other arithmetic  26.2 us (10%)
  blocking collectives  24.1 us (9%)
  between operations  15.7 us (6%)
  starting transfers between devices  4.41 us (2%)
    unnamed x3, waiting for transfers between devices  79 us
    unnamed x40, local copies, waits for them, and re-layouts  19 us
    all_gather x1, waiting for transfers between devices, body(): rows_piece = lax.all_gather(resid_half, 'dir', axis=0, tiled=True)  18.7 us
    dot_general x1, matrix products, body(): geometry = jnp.einsum('mcp,ck->pmk', uv_each, source_lm, precision=highest)  14.2 us
    psum x1, blocking collectives, body(): total_sq = lax.psum(jnp.sum(smooth * smooth), 'dir')  12.4 us
    psum x1, blocking collectives, body(): total_grad = lax.psum(local_grad, 'freq')  11.7 us
    all_to_all x1, waiting for transfers between devices, body(): lax.all_to_all(jnp.stack(jnp.split(packed_rows, lax.axis_size('dir'), axi...  8.67 us
    dot_general x1, matrix products, body(): jnp.einsum('rmwq,qmwk->rmk', rows_piece, forward_mat, preferred_element_t...  7.73 us
  transfers between devices with their start and end apart: 3, of which 3 were waited for; matrix products, arithmetic and copies ran while one was open for 8% of the time, Pallas kernels for 0%

profile of v1, /device:TPU:0, one launch (start us, length us, event | category | flops | bytes accessed | tf_op | source)
XLA Modules:
  0.0 256.7 jit_solution(3317104095394393499)
XLA Ops:
  8.8 5.5 %copy.27 = f32[2,2,2,512,384]{3,4,1,0,2:T(8,128)} copy(bf16[2,2,2,512,384]{4,3,2,1,0:T(8,128)(2,1)} %param.17) | data formatting | bytes 9437184 | tf_op jit(solution)/shard_map/convert_element_type | solution.py:44
  14.9 14.2 %fusion.54 = (f32[512,4,384]{0,2,1:T(8,128)S(1)}, f32[512,4,384]{0,2,1:T(8,128)S(1)}) fusion(f32[4,2,512]{2,1,0:T(2,128)S(1)} %bitcast.107, f32[2,384]{1,0:T(2,128)S(1)} %copy-done.11, f32[4]{0:T(128)S(1)} %get-tuple-element.16, f32[4]{0:T(128)S(1)} %div.26, f32[512,384]{0,1:T(8,128)S(1)} %convolution_bitcast_fusion), kind=kOutput, calls=%fused_computation.82 | convolution fusion | flops 21233664 | bytes 7097376 | tf_op jit(solution)/shard_map/mcp,ck->pmk/dot_general | solution.py:39
  29.1 3.2 %fusion.53 = (bf16[512,4,384]{0,2,1:T(8,128)(2,1)}, bf16[512,4,384]{0,2,1:T(8,128)(2,1)S(1)}, bf16[512,4,1,384]{0,3,1,2:T(8,128)(2,1)}, bf16[512,4,384]{0,2,1:T(8,128)(2,1)S(1)}) fusion(f32[512,4,384]{0,2,1:T(8,128)S(1)} %get-tuple-element.12, f32[4,2,512,384]{2,3,0,1:T(8,128)S(1)} %bitcast.101, f32[512,4,384]{0,2,1:T(8,128)S(1)} %get-tuple-element.13, ...), kind=kLoop, calls=%fused_computation.81 | loop fusion | flops 9437184 | bytes 18875904 | tf_op jit(solution)/shard_map/neg | solution.py:78
  32.5 2.1 fusion.30
  34.6 3.4 %multiply_bitcast_fusion = f32[512,4,512]{0,2,1:T(8,128)} fusion(f32[4,512,512]{2,1,0:T(8,128)S(1)} %fusion.30, bf16[512,4,384]{0,2,1:T(8,128)(2,1)S(1)} %get-tuple-element.5, bf16[512,4,384]{0,2,1:T(8,128)(2,1)S(1)} %neg.16, bf16[512,4,384]{0,2,1:T(8,128)(2,1)S(1)} %get-tuple-element.7), kind=kOutput, calls=%fused_computation.8 | convolution fusion | flops 1625292800 | bytes 13107200 | tf_op jit(solution)/shard_map/pmk,qmk->pmq/dot_general | solution.py:55
  38.1 5.5 %copy.32 = f32[512,4,512]{2,1,0:T(4,128)} copy(f32[512,4,512]{0,2,1:T(8,128)} %multiply_bitcast_fusion) | data formatting | bytes 8388608 | tf_op jit(solution)/shard_map/mul | solution.py:57
  48.3 79.0 %all-reduce.3.cloned.1.call-done = f32[512,4,512]{2,1,0:T(4,128)} async-done(((f32[512,4,512]{2,1,0:T(4,128)}), f32[512,4,512]{2,1,0:T(4,128)}) %all-reduce.3.cloned.1.call-update) | async-done | bytes 4194320
  130.6 1.7 fusion.42
  140.9 3.0 %reshape.110 = f32[8,1,16384]{2,1,0:T(1,128)} reshape(f32[8,64,4,64]{3,2,1,0:T(4,128)} %fusion.37) | data formatting | bytes 1048576
  144.0 4.3 %all-to-all-start = ((f32[8,1,16384]{2,1,0:T(1,128)}), f32[8,1,16384]{2,1,0:T(1,128)}, u32[]{:S(2)}, u32[]{:S(2)}) async-start(f32[8,1,16384]{2,1,0:T(1,128)} %reshape.110), calls=%async_computation | async-start | bytes 1048576 | tf_op jit(solution)/shard_map/all_to_all | solution.py:60
  149.4 8.7 %all-to-all-done = f32[8,1,16384]{2,1,0:T(1,128)} async-done(((f32[8,1,16384]{2,1,0:T(1,128)}), f32[8,1,16384]{2,1,0:T(1,128)}, u32[]{:S(2)}, u32[]{:S(2)}) %all-to-all-start) | async-done | bytes 524320 | tf_op jit(solution)/shard_map/all_to_all | solution.py:60
  158.5 2.9 %reduce = f32[8,16384]{1,0:T(8,128)S(1)} reduce(f32[8,1,16384]{2,1,0:T(1,128)} %all-to-all-done, f32[]{:T(128)} %broadcast.60), dimensions={1}, to_apply=%all_to_all.3.reduce_sub_computation | reduce | bytes 1048580 | tf_op jit(solution)/shard_map/all_to_all | solution.py:60
  163.1 2.4 copy.50
  167.7 1.8 fusion.33
  170.5 4.4 %maximum_negate_fusion = bf16[512,4,1,768]{0,3,1,2:T(8,128)(2,1)} fusion(bf16[512,4,1,384]{0,3,1,2:T(8,128)(2,1)} %get-tuple-element.6, bf16[512,4,1,384]{0,3,1,2:T(8,128)(2,1)} %bitcast.102), kind=kLoop, calls=%fused_computation.29 | loop fusion | flops 7864320 | bytes 6291456 | tf_op jit(solution)/shard_map/neg | solution.py:77
  175.9 3.8 %fusion.29 = (bf16[512,4,1,768]{0,3,1,2:T(8,128)(2,1)}, bf16[512,4,1,768]{0,3,1,2:T(8,128)(2,1)}, bf16[512,4,1,768]{0,3,1,2:T(8,128)(2,1)}) fusion(bf16[512,4,384]{0,2,1:T(8,128)(2,1)S(1)} %copy-done.2, bf16[512,4,384]{0,2,1:T(8,128)(2,1)S(1)} %get-tuple-element.7, bf16[512,4,384]{0,2,1:T(8,128)(2,1)S(1)} %copy-done.4), kind=kLoop, calls=%fused_computation.34 | loop fusion | flops 17301504 | bytes 14155776 | tf_op jit(solution)/shard_map/stack | solution.py:77
  179.6 2.6 %stack.78 = f32[64,2,2,1,512]{4,3,2,1,0:T(1,128)} reshape(f32[64,4,512]{2,1,0:T(4,128)} %copy-done.5) | data formatting | bytes 1048576 | tf_op jit(solution)/shard_map/stack | solution.py:66
  183.7 3.9 %fusion.31 = f32[64,2,2,2,512]{4,3,2,1,0:T(2,128)} fusion(f32[64,2,2,2,512]{4,3,2,1,0:T(2,128)} %param.10, f32[64,2,2,1,512]{4,3,2,1,0:T(1,128)} %stack.79, f32[64,2,2,1,512]{4,3,2,1,0:T(1,128)} %stack.78, f32[64,2,2,512]{3,2,1,0:T(2,128)} %broadcast_multiply_fusion.1), kind=kLoop, calls=%fused_computation.38 | loop fusion | flops 786432 | bytes 3670016 | tf_op jit(solution)/shard_map/mul | solution.py:75
  187.7 18.7 %all-gather.2.cloned.1.call-done = bf16[512,4,2,512]{3,1,2,0:T(4,128)(2,1)} async-done(((bf16[64,4,2,512]{3,1,2,0:T(4,128)(2,1)}), bf16[512,4,2,512]{3,1,2,0:T(4,128)(2,1)}) %all-gather.2.cloned.1.call-update) | async-done | bytes 4194320 | tf_op jit(solution)/shard_map/all_gather | solution.py:81
  206.3 7.7 %fusion.24 = f32[512,4,768]{0,2,1:T(8,128)S(1)} fusion(bf16[512,4,2,512]{3,1,2,0:T(4,128)(2,1)} %all-gather.2.cloned.1.call-done, bf16[512,4,1,768]{0,3,1,2:T(8,128)(2,1)} %maximum_negate_fusion, bf16[512,4,1,768]{0,3,1,2:T(8,128)(2,1)} %get-tuple-element.10), kind=kOutput, calls=%fused_computation.33 | convolution fusion | flops 3224371200 | bytes 16777216 | tf_op jit(solution)/shard_map/rmwq,qmwk->rmk/dot_general | solution.py:82
  214.1 6.8 %fusion.19 = f32[512,4,768]{0,2,1:T(8,128)S(1)} fusion(bf16[512,4,2,512]{3,1,2,0:T(4,128)(2,1)} %all-gather.2.cloned.1.call-done, bf16[512,4,1,768]{0,3,1,2:T(8,128)(2,1)S(1)} %copy-done.6, bf16[512,4,1,768]{0,3,1,2:T(8,128)(2,1)} %get-tuple-element.14), kind=kOutput, calls=%fused_computation.32 | convolution fusion | flops 3224371200 | bytes 16777216 | tf_op jit(solution)/shard_map/rmwp,rmwk->pmk/dot_general | solution.py:85
  220.9 1.9 fusion.16
  223.2 11.7 %psum.14 = f32[2,512]{1,0:T(2,128)S(1)} all-reduce(f32[2,512]{1,0:T(2,128)S(1)} %fusion.36), channel_id=1, replica_groups=mesh['dir'=8,'freq'=4] {'freq'}, use_global_device_ids=true, to_apply=%region_2.0 | all-reduce | flops 1024 | bytes 8192 | tf_op jit(solution)/shard_map/psum | solution.py:96
  236.1 12.4 %psum.15 = f32[]{:T(128)} all-reduce(f32[]{:T(128)} %get-tuple-element.18), channel_id=1, replica_groups=mesh['dir'=8,'freq'=4] {'dir'}, use_global_device_ids=true, to_apply=%region_4.0 | all-reduce | flops 1 | bytes 8 | tf_op jit(solution)/shard_map/psum | solution.py:98
  (65 shorter events, 29.6 us)
Async XLA Ops:
  7.2 227.7 %copy-start = (f32[512,512]{1,0:T(8,128)S(1)}, f32[512,512]{1,0:T(8,128)}, u32[]{:S(2)}) copy-start(f32[512,512]{1,0:T(8,128)} %param.13) | copy-start | bytes 3145732
  7.2 120.1 %all-reduce.3.cloned.1.call-start = ((), (), s32[]{:S(2)}) async-start(), calls=%async_computation.2 | async-start | bytes 8388608
  8.8 5.5 %copy-start.8 = (f32[2,512]{1,0:T(2,128)S(1)}, f32[2,512]{1,0:T(2,128)}, u32[]{:S(2)}) copy-start(f32[2,512]{1,0:T(2,128)} %param.12) | copy-start | bytes 12292
  8.8 5.5 %copy-start.9 = (s32[384]{0:T(512)S(1)}, s32[384]{0:T(512)}, u32[]{:S(2)}) copy-start(s32[384]{0:T(512)} %param.18) | copy-start | bytes 4612
  8.8 6.0 %copy-start.10 = (f32[2,2,512]{2,1,0:T(2,128)S(1)}, f32[2,2,512]{2,1,0:T(2,128)}, u32[]{:S(2)}) copy-start(f32[2,2,512]{2,1,0:T(2,128)} %param.14) | copy-start | bytes 24580
  8.8 6.0 %copy-start.11 = (f32[2,384]{1,0:T(2,128)S(1)}, f32[2,384]{1,0:T(2,128)}, u32[]{:S(2)}) copy-start(f32[2,384]{1,0:T(2,128)} %param.15) | copy-start | bytes 9220
  14.8 14.2 %slice-start = ((s8[6291456]{0:T(1024)(128)(4,1)}), s8[4194304]{0:T(1024)(128)(4,1)S(1)}, s32[]{:S(2)}) async-start(s8[6291456]{0:T(1024)(128)(4,1)} %bitcast.99), calls=%async_computation.3 | async-start | bytes 8388608
  14.9 14.2 %slice-start.1 = ((s8[6291456]{0:T(1024)(128)(4,1)}), s8[2097152]{0:T(1024)(128)(4,1)S(1)}, s32[]{:S(2)}) async-start(s8[6291456]{0:T(1024)(128)(4,1)} %bitcast.99), calls=%async_computation.4 | async-start | bytes 4194304
  32.2 2.4 copy-start.1
  43.5 0.9 copy-start.7
  43.6 3.5 %copy-start.12 = (u32[32]{0:T(128)S(1)}, u32[32]{0:T(128)}, u32[]{:S(2)}) copy-start(u32[32]{0:T(128)} %constant.30) | copy-start | bytes 388
  144.0 14.1 %all-to-all-start = ((f32[8,1,16384]{2,1,0:T(1,128)}), f32[8,1,16384]{2,1,0:T(1,128)}, u32[]{:S(2)}, u32[]{:S(2)}) async-start(f32[8,1,16384]{2,1,0:T(1,128)} %reshape.110), calls=%async_computation | async-start | bytes 1048576 | tf_op jit(solution)/shard_map/all_to_all | solution.py:60
  148.3 58.0 %all-gather.2.cloned.1.call-start = ((), (), s32[]{:S(2)}) async-start(), calls=%async_computation.1 | async-start | bytes 4718592 | tf_op jit(solution)/shard_map/all_gather | solution.py:81
  166.9 0.8 copy-start.5
  170.5 5.4 %copy-start.2 = (bf16[512,4,384]{0,2,1:T(8,128)(2,1)S(1)}, bf16[512,4,384]{0,2,1:T(8,128)(2,1)}, u32[]{:S(2)}) copy-start(bf16[512,4,384]{0,2,1:T(8,128)(2,1)} %copy-done.1) | copy-start | bytes 4718596
  170.5 5.4 %copy-start.4 = (bf16[512,4,384]{0,2,1:T(8,128)(2,1)S(1)}, bf16[512,4,384]{0,2,1:T(8,128)(2,1)}, u32[]{:S(2)}) copy-start(bf16[512,4,384]{0,2,1:T(8,128)(2,1)} %get-tuple-element.4) | copy-start | bytes 4718596
  206.3 7.7 %copy-start.6 = (bf16[512,4,1,768]{0,3,1,2:T(8,128)(2,1)S(1)}, bf16[512,4,1,768]{0,3,1,2:T(8,128)(2,1)}, u32[]{:S(2)}) copy-start(bf16[512,4,1,768]{0,3,1,2:T(8,128)(2,1)} %get-tuple-element.11) | copy-start | bytes 9437188
  214.1 6.8 %copy-start.3 = (bf16[512,4,384]{0,2,1:T(8,128)(2,1)S(1)}, bf16[512,4,384]{0,2,1:T(8,128)(2,1)}, u32[]{:S(2)}) copy-start(bf16[512,4,384]{0,2,1:T(8,128)(2,1)} %copy-done.1) | copy-start | bytes 4718596
Sparse Core Ops, SparseCore 0:
  43.7 83.5 all-reduce.2
  170.6 35.6 all-gather.1
